TPU v7x, 32 devices: a whole 2x2x4 slice. The times are simulated.
32 devices in a mesh: expert: 8 (over y, x, core), shard: 4 (over z).
Axes of the slice: x: 2, y: 2, z: 4, core: 2. Of those that a mesh axis runs over, the one named last changes fastest.
Arguments:
- inputs: bfloat16 [6304, 768], P(('expert', 'shard')), may hold values from -6 to 6
- routes: int32 [6304, 2], P(('expert', 'shard')), may hold values from 0 to 15, all different within a row; in each aligned block of 197 rows (0 to 196, 197 to 393, ...) at most 39 rows name the same one
- ln1_gain: bfloat16 [768], P(('expert', 'shard')), may hold values from 0.099609375 to 1.8984375
- ln1_bias: bfloat16 [768], P(('expert', 'shard')), may hold values from -3 to 3
- w_qkv: bfloat16 [768, 2304], P(('expert', 'shard')), may hold values from -0.21875 to 0.21875
- w_attn_out: bfloat16 [768, 768], P(('expert', 'shard')), may hold values from -0.625 to 0.625
- ln2_gain: bfloat16 [768], P(('expert', 'shard')), may hold values from 0.099609375 to 1.8984375
- ln2_bias: bfloat16 [768], P(('expert', 'shard')), may hold values from -3 to 3
- w_router: bfloat16 [768, 16], P(('expert', 'shard')), may hold values from -0.109375 to 0.109375
- w_in: bfloat16 [16, 768, 3072], P('expert', None, 'shard'), may hold values from -0.21875 to 0.21875
- w_expert_out: bfloat16 [16, 3072, 768], P('expert', 'shard'), may hold values from -1.25 to 1.25
- cotangent: bfloat16 [6304, 768], P(('expert', 'shard')), may hold values from -6 to 6
Outputs:
- outputs: bfloat16 [6304, 768], P(('expert', 'shard'))
- grad_inputs: float32 [6304, 768], P(('expert', 'shard'))
- grad_ln1_gain: float32 [768], P(('expert', 'shard'))
- grad_ln1_bias: float32 [768], P(('expert', 'shard'))
- grad_w_qkv: float32 [768, 2304], P(('expert', 'shard'))
- grad_w_attn_out: float32 [768, 768], P(('expert', 'shard'))
- grad_ln2_gain: float32 [768], P(('expert', 'shard'))
- grad_ln2_bias: float32 [768], P(('expert', 'shard'))
- grad_w_router: float32 [768, 16], P(('expert', 'shard'))
- grad_w_in: float32 [16, 768, 3072], P('expert', None, 'shard')
- grad_w_expert_out: float32 [16, 3072, 768], P('expert', 'shard')
Inputs may be any that keep to these rules, and one draw needn't show every extreme that they name: `routes`: each token names two different experts; among the 197 tokens of one device no expert is named more than 39 times, and in every draw some expert is named exactly 39 times by one device's tokens.
All inputs are finite; a program needn't handle non-finite values.
Results may differ from a plain program's by a relative error of at most 0.018.
Values may be sent and summed in bfloat16 or wider, within the bound.
No kernel may reach another device: no remote copies, remote signals or barrier semaphores. Data moves between devices by JAX's collectives and lax.ppermute only.
A program may use at most 192 MiB of HBM per device.

v0:
```python
from functools import partial
import jax
import jax.numpy as jnp
from jax import lax
from jax.sharding import PartitionSpec as P

HEADS = 12
HEAD_DIM = 64
EXP_DEV = 2
SEQ = 197
EPS = 1e-06


def layer_norm(values, gain_vec, bias_vec):
    average = jnp.mean(values, axis=-1, keepdims=True)
    centred = values - average
    inverse = lax.rsqrt(jnp.mean(centred * centred, axis=-1, keepdims=True) + EPS)
    unit_vals = centred * inverse
    return (unit_vals * gain_vec + bias_vec, unit_vals, inverse)


def norm_back(grad_out, unit_vals, inverse, gain_vec):
    scaled = grad_out * gain_vec
    centred = (
        scaled
        - jnp.mean(scaled, axis=-1, keepdims=True)
        - unit_vals * jnp.mean(scaled * unit_vals, axis=-1, keepdims=True)
    )
    return (inverse * centred, jnp.sum(grad_out * unit_vals, axis=0), jnp.sum(grad_out, axis=0))


def split_heads(packed):
    shaped = packed.reshape(packed.shape[0], packed.shape[1], 3, HEADS, HEAD_DIM)
    return (shaped[:, :, 0], shaped[:, :, 1], shaped[:, :, 2])


def attn_probs(queries, keys_part):
    scores = jnp.einsum(
        "iqhd,ikhd->ihqk", queries, keys_part, preferred_element_type=jnp.float32
    ) * HEAD_DIM ** (-0.5)
    exponent = jnp.exp(scores)
    return exponent / jnp.sum(exponent, axis=-1, keepdims=True)


def attention_forward(packed):
    queries, keys_part, values_part = split_heads(packed)
    probs_b = attn_probs(queries, keys_part).astype(jnp.bfloat16)
    context = jnp.einsum(
        "ihqk,ikhd->iqhd", probs_b, values_part, preferred_element_type=jnp.float32
    )
    return context.astype(jnp.bfloat16).reshape(packed.shape[0], packed.shape[1], HEADS * HEAD_DIM)


def attention_backward(packed, d_context):
    queries, keys_part, values_part = split_heads(packed)
    probs = attn_probs(queries, keys_part)
    probs_b = probs.astype(jnp.bfloat16)
    d_heads = d_context.reshape(packed.shape[0], packed.shape[1], HEADS, HEAD_DIM)
    d_values = jnp.einsum("ihqk,iqhd->ikhd", probs_b, d_heads, preferred_element_type=jnp.float32)
    d_probs = jnp.einsum(
        "iqhd,ikhd->ihqk", d_heads, values_part, preferred_element_type=jnp.float32
    )
    row_dot = jnp.sum(probs * d_probs, axis=-1, keepdims=True)
    d_scores = (probs * (d_probs - row_dot)).astype(jnp.bfloat16)
    scale = HEAD_DIM ** (-0.5)
    d_queries = (
        jnp.einsum("ihqk,ikhd->iqhd", d_scores, keys_part, preferred_element_type=jnp.float32)
        * scale
    )
    d_keys = (
        jnp.einsum("ihqk,iqhd->ikhd", d_scores, queries, preferred_element_type=jnp.float32) * scale
    )
    stacked = jnp.stack([d_queries, d_keys, d_values], axis=2)
    return stacked.astype(jnp.bfloat16).reshape(
        packed.shape[0], packed.shape[1], 3 * HEADS * HEAD_DIM
    )


def expert_forward(arrived, weight_in, weight_out):
    pre_act = jnp.einsum("emd,edf->emf", arrived, weight_in, preferred_element_type=jnp.float32)
    hidden_act = jax.nn.gelu(pre_act, approximate=True).astype(jnp.bfloat16)
    partial_out = jnp.einsum(
        "emf,efd->emd", hidden_act, weight_out, preferred_element_type=jnp.float32
    )
    return (partial_out, pre_act, hidden_act)


def expert_backward(arrived, grad_rows, pre_act, hidden_act, weight_in, weight_out):
    d_hidden_act = jnp.einsum(
        "emd,efd->emf", grad_rows, weight_out, preferred_element_type=jnp.float32
    )
    _, pullback = jax.vjp(partial(jax.nn.gelu, approximate=True), pre_act)
    d_pre = pullback(d_hidden_act)[0].astype(jnp.bfloat16)
    grad_out_w = jnp.einsum(
        "emf,emd->efd", hidden_act, grad_rows, preferred_element_type=jnp.float32
    )
    grad_in_w = jnp.einsum("emd,emf->edf", arrived, d_pre, preferred_element_type=jnp.float32)
    back_rows = jnp.einsum("emf,edf->emd", d_pre, weight_in, preferred_element_type=jnp.float32)
    return (back_rows, grad_in_w, grad_out_w)


def local(
    inputs,
    routes,
    ln1_gain,
    ln1_bias,
    w_qkv,
    w_attn_out,
    ln2_gain,
    ln2_bias,
    w_router,
    w_in,
    w_expert_out,
    cotangent,
):
    row_count = inputs.shape[0]
    width = inputs.shape[1]
    experts_count = lax.axis_size("expert")
    shard_count = lax.axis_size("shard")
    total_experts = EXP_DEV * experts_count
    capacity = max(2, 16 * row_count // (5 * total_experts))
    images = row_count // SEQ
    (
        full_ln1_gain,
        full_ln1_bias,
        full_qkv,
        full_attn_out,
        full_ln2_gain,
        full_ln2_bias,
        full_router,
    ) = (
        lax.all_gather(ln1_gain, ("expert", "shard"), axis=0, tiled=True),
        lax.all_gather(ln1_bias, ("expert", "shard"), axis=0, tiled=True),
        lax.all_gather(w_qkv, ("expert", "shard"), axis=0, tiled=True),
        lax.all_gather(w_attn_out, ("expert", "shard"), axis=0, tiled=True),
        lax.all_gather(ln2_gain, ("expert", "shard"), axis=0, tiled=True),
        lax.all_gather(ln2_bias, ("expert", "shard"), axis=0, tiled=True),
        lax.all_gather(w_router, ("expert", "shard"), axis=0, tiled=True),
    )
    gain_one = full_ln1_gain.astype(jnp.float32)
    gain_two = full_ln2_gain.astype(jnp.float32)
    features = inputs.astype(jnp.float32)
    normed1, unit_one, inverse_one = layer_norm(
        features, gain_one, full_ln1_bias.astype(jnp.float32)
    )
    narrow_one = normed1.astype(jnp.bfloat16)
    packed = jnp.dot(narrow_one, full_qkv, preferred_element_type=jnp.float32).astype(jnp.bfloat16)
    packed_images = packed.reshape(images, SEQ, 3 * width)
    context = attention_forward(packed_images).reshape(row_count, width)
    hidden = features + jnp.dot(context, full_attn_out, preferred_element_type=jnp.float32)
    normed2, unit_two, inverse_two = layer_norm(hidden, gain_two, full_ln2_bias.astype(jnp.float32))
    narrow_two = normed2.astype(jnp.bfloat16)
    logits = jnp.dot(narrow_two, full_router, preferred_element_type=jnp.float32)
    exponent = jnp.exp(logits)
    router_probs = exponent / jnp.sum(exponent, axis=-1, keepdims=True)
    route_table = (
        routes[:, :, None] == jnp.arange(total_experts, dtype=jnp.int32)[None, None, :]
    ).astype(jnp.float32)
    gate_vals = jnp.sum(route_table * router_probs[:, None, :], axis=-1)
    flat_routes = routes.reshape(-1)
    expert_table = (
        flat_routes[:, None] == jnp.arange(total_experts, dtype=jnp.int32)[None, :]
    ).astype(jnp.int32)
    slot_ranks = jnp.sum((jnp.cumsum(expert_table, axis=0) - 1) * expert_table, axis=1)
    owner_index = flat_routes // EXP_DEV
    local_index = flat_routes % EXP_DEV
    slot_place = (local_index * experts_count + owner_index) * capacity + slot_ranks
    buffer_rows = EXP_DEV * experts_count * capacity
    send_buffer = (
        jnp.zeros((buffer_rows, width), jnp.bfloat16)
        .at[slot_place]
        .set(jnp.repeat(narrow_two, 2, axis=0))
    )
    send_buffer = send_buffer.reshape(EXP_DEV, experts_count, capacity, width)
    copies = jnp.broadcast_to(
        send_buffer[:, :, None], (EXP_DEV, experts_count, shard_count, capacity, width)
    )
    copies = copies.reshape(EXP_DEV, experts_count * shard_count, capacity, width)
    arrived = lax.all_to_all(
        copies, ("expert", "shard"), split_axis=1, concat_axis=1, tiled=True
    ).reshape(EXP_DEV, -1, width)
    partial_out, pre_act, hidden_act = expert_forward(arrived, w_in, w_expert_out)
    returned = lax.all_to_all(
        partial_out.astype(jnp.bfloat16).reshape(
            EXP_DEV, experts_count * shard_count, capacity, width
        ),
        ("expert", "shard"),
        split_axis=1,
        concat_axis=1,
        tiled=True,
    )
    expert_buffer = jnp.sum(
        returned.reshape(EXP_DEV, experts_count, shard_count, capacity, width).astype(jnp.float32),
        axis=2,
    ).astype(jnp.bfloat16)
    expert_vals = (
        expert_buffer.reshape(buffer_rows, width)[slot_place]
        .reshape(row_count, 2, width)
        .astype(jnp.float32)
    )
    outputs = (hidden + jnp.sum(gate_vals[:, :, None] * expert_vals, axis=1)).astype(jnp.bfloat16)
    grad_out = cotangent.astype(jnp.float32)
    d_expert = (
        (gate_vals[:, :, None] * grad_out[:, None, :])
        .astype(jnp.bfloat16)
        .reshape(2 * row_count, width)
    )
    grad_buffer = jnp.zeros((buffer_rows, width), jnp.bfloat16).at[slot_place].set(d_expert)
    grad_buffer = grad_buffer.reshape(EXP_DEV, experts_count, capacity, width)
    grad_copies = jnp.broadcast_to(
        grad_buffer[:, :, None], (EXP_DEV, experts_count, shard_count, capacity, width)
    )
    grad_copies = grad_copies.reshape(EXP_DEV, experts_count * shard_count, capacity, width)
    grad_rows = lax.all_to_all(
        grad_copies, ("expert", "shard"), split_axis=1, concat_axis=1, tiled=True
    ).reshape(EXP_DEV, -1, width)
    back_rows, grad_w_in, grad_w_expert_out = expert_backward(
        arrived, grad_rows, pre_act, hidden_act, w_in, w_expert_out
    )
    back_returned = lax.all_to_all(
        back_rows.astype(jnp.bfloat16).reshape(
            EXP_DEV, experts_count * shard_count, capacity, width
        ),
        ("expert", "shard"),
        split_axis=1,
        concat_axis=1,
        tiled=True,
    )
    back_buffer = jnp.sum(
        back_returned.reshape(EXP_DEV, experts_count, shard_count, capacity, width).astype(
            jnp.float32
        ),
        axis=2,
    ).astype(jnp.bfloat16)
    back_vals = (
        back_buffer.reshape(buffer_rows, width)[slot_place]
        .reshape(row_count, 2, width)
        .astype(jnp.float32)
    )
    d_gate = jnp.sum(expert_vals * grad_out[:, None, :], axis=-1)
    d_probs = jnp.sum(route_table * d_gate[:, :, None], axis=1)
    d_logits = router_probs * (d_probs - jnp.sum(router_probs * d_probs, axis=-1, keepdims=True))
    grad_router = jnp.dot(
        narrow_two.astype(jnp.float32).T, d_logits, precision=lax.Precision.HIGHEST
    )
    d_normed2 = (
        back_vals[:, 0]
        + back_vals[:, 1]
        + jnp.dot(d_logits, full_router.astype(jnp.float32).T, precision=lax.Precision.HIGHEST)
    )
    d_norm_two, grad_gain_two, grad_bias_two = norm_back(d_normed2, unit_two, inverse_two, gain_two)
    d_hidden = grad_out + d_norm_two
    d_hidden_b = d_hidden.astype(jnp.bfloat16)
    grad_attn_out = jnp.dot(context.T, d_hidden_b, preferred_element_type=jnp.float32)
    d_context = jnp.dot(d_hidden_b, full_attn_out.T, preferred_element_type=jnp.float32).astype(
        jnp.bfloat16
    )
    d_packed = attention_backward(packed_images, d_context.reshape(images, SEQ, width)).reshape(
        row_count, 3 * width
    )
    grad_qkv = jnp.dot(narrow_one.T, d_packed, preferred_element_type=jnp.float32)
    d_normed1 = jnp.dot(d_packed, full_qkv.T, preferred_element_type=jnp.float32)
    d_norm_one, grad_gain_one, grad_bias_one = norm_back(d_normed1, unit_one, inverse_one, gain_one)
    grad_inputs = d_hidden + d_norm_one
    shard_grads = (
        lax.psum_scatter(grad_gain_one, ("expert", "shard"), scatter_dimension=0, tiled=True),
        lax.psum_scatter(grad_bias_one, ("expert", "shard"), scatter_dimension=0, tiled=True),
        lax.psum_scatter(grad_qkv, ("expert", "shard"), scatter_dimension=0, tiled=True),
        lax.psum_scatter(grad_attn_out, ("expert", "shard"), scatter_dimension=0, tiled=True),
        lax.psum_scatter(grad_gain_two, ("expert", "shard"), scatter_dimension=0, tiled=True),
        lax.psum_scatter(grad_bias_two, ("expert", "shard"), scatter_dimension=0, tiled=True),
        lax.psum_scatter(grad_router, ("expert", "shard"), scatter_dimension=0, tiled=True),
    )
    return (
        outputs,
        grad_inputs,
        shard_grads[0],
        shard_grads[1],
        shard_grads[2],
        shard_grads[3],
        shard_grads[4],
        shard_grads[5],
        shard_grads[6],
        grad_w_in,
        grad_w_expert_out,
    )


def solution(mesh):
    placed = (
        P(("expert", "shard"), None),
        P(("expert", "shard"), None),
        P(("expert", "shard")),
        P(("expert", "shard")),
        P(("expert", "shard"), None),
        P(("expert", "shard"), None),
        P(("expert", "shard")),
        P(("expert", "shard")),
        P(("expert", "shard"), None),
        P("expert", None, "shard"),
        P("expert", "shard", None),
        P(("expert", "shard"), None),
    )
    return jax.shard_map(
        local,
        mesh=mesh,
        in_specs=placed,
        out_specs=(
            P(("expert", "shard"), None),
            P(("expert", "shard"), None),
            P(("expert", "shard")),
            P(("expert", "shard")),
            P(("expert", "shard"), None),
            P(("expert", "shard"), None),
            P(("expert", "shard")),
            P(("expert", "shard")),
            P(("expert", "shard"), None),
            P("expert", None, "shard"),
            P("expert", "shard", None),
        ),
        check_vma=False,
    )
```

profile of v0, /device:TPU:0, one launch (start us, length us, event | category | flops | bytes accessed | tf_op | source)
XLA Modules:
  0.0 836.1 jit_solution(15612730943233927890)
XLA Ops:
  13.1 42.3 %all-reduce.11 = (bf16[768]{0:T(1024)(128)(2,1)S(1)}, bf16[768]{0:T(1024)(128)(2,1)S(1)}, bf16[768]{0:T(1024)(128)(2,1)S(1)}, bf16[768]{0:T(1024)(128)(2,1)S(1)}) all-reduce(bf16[768]{0:T(1024)(128)(2,1)S(1)} %dynamic-update-slice.1, bf16[768]{0:T(1024)(128)(2,1)S(1)} %dynamic-update-slice, ...), channel_id=1, replica_groups=mesh['expert'=8,'shard'=4] {'expert','shard'}, use_global_device_ids=true, to_apply=%add.2 | all-reduce | flops 3072 | bytes 12288
  60.5 13.1 %all-gather.4.cloned.1.call-done = bf16[768,2304]{1,0:T(8,128)(2,1)} async-done(((bf16[24,2304]{1,0:T(8,128)(2,1)}), bf16[768,2304]{1,0:T(8,128)(2,1)}) %all-gather.4.cloned.1.call-update) | async-done | bytes 3538960 | tf_op jit(solution)/shard_map/all_gather | solution.py:134
  73.6 4.0 convolution_convert_fusion.2
  77.6 1.5 copy.116
  81.4 2.4 convolution_convert_fusion.4
  83.8 45.4 %all-gather.6.cloned.1.call-done = bf16[768,768]{1,0:T(8,128)(2,1)} async-done(((bf16[24,768]{1,0:T(8,128)(2,1)}), bf16[768,768]{1,0:T(8,128)(2,1)}) %all-gather.6.cloned.1.call-update) | async-done | bytes 1179664 | tf_op jit(solution)/shard_map/all_gather | solution.py:135
  129.2 1.9 fusion.62
  133.4 2.6 reshape.387
  136.0 3.9 scatter_custom_fusion
  139.9 2.4 broadcast_in_dim.11
  142.4 2.2 copy.124
  144.6 3.9 broadcast_in_dim.12
  148.4 3.7 all-to-all-start
  152.2 145.9 %all-gather = bf16[32,24,16]{1,2,0:T(8,128)(2,1)S(1)} all-gather(bf16[1,24,16]{1,2,0:T(8,128)(2,1)S(1)} %bitcast.120), channel_id=1, replica_groups=mesh['expert'=8,'shard'=4] {'expert','shard'}, dimensions={0}, use_global_device_ids=true | all-gather | bytes 25344 | tf_op jit(solution)/shard_map/all_gather | solution.py:138
  298.3 2.3 mul.281
  300.6 3.0 mul.282
  305.1 4.0 scatter_custom_fusion.1
  309.1 2.4 broadcast_in_dim.13
  311.5 3.1 copy.129
  314.6 5.1 broadcast_in_dim.14
  319.7 3.8 all-to-all-start.2
  323.5 6.0 fusion.15
  329.5 4.9 convolution_convert_fusion.1
  334.4 15.0 %copy.145 = bf16[2,1248,768]{2,0,1:T(2,128)(2,1)} copy(bf16[2,1248,768]{2,1,0:T(8,128)(2,1)S(1)} %convolution_convert_fusion.1) | data formatting | bytes 7667712 | tf_op jit(solution)/shard_map/reshape | solution.py:184
  349.5 58.7 %all-to-all-done.2 = bf16[2,32,39,768]{3,0,2,1:T(2,128)(2,1)} async-done(((bf16[2,32,39,768]{3,0,2,1:T(2,128)(2,1)}), bf16[2,32,39,768]{3,0,2,1:T(2,128)(2,1)}, u32[]{:S(2)}, u32[]{:S(2)}) %all-to-all-start.2) | async-done | bytes 3833888 | tf_op jit(solution)/shard_map/all_to_all | solution.py:214
  408.2 5.9 all-to-all-start.1
  414.1 10.3 %fusion.6 = bf16[2,1248,768]{2,1,0:T(8,128)(2,1)S(1)} fusion(f32[2,1248,768]{2,1,0:T(8,128)} %copy-done.28, bf16[2,768,768]{2,1,0:T(8,128)(2,1)S(1)} %copy-done, bf16[2,1248,768]{2,0,1:T(2,128)(2,1)} %bitcast.16), kind=kOutput, calls=%fused_computation.12 | convolution fusion | flops 2982739968 | bytes 17694720 | tf_op jit(solution)/shard_map/emd,efd->emf/dot_general | solution.py:89
  424.5 3.4 convolution_convert_fusion
  427.9 15.0 %copy.147 = bf16[2,1248,768]{2,0,1:T(2,128)(2,1)} copy(bf16[2,1248,768]{2,1,0:T(8,128)(2,1)S(1)} %convolution_convert_fusion) | data formatting | bytes 7667712 | tf_op jit(solution)/shard_map/reshape | solution.py:221
  443.0 55.8 %all-to-all-done.1 = bf16[2,32,39,768]{3,0,2,1:T(2,128)(2,1)} async-done(((bf16[2,32,39,768]{3,0,2,1:T(2,128)(2,1)}), bf16[2,32,39,768]{3,0,2,1:T(2,128)(2,1)}, u32[]{:S(2)}, u32[]{:S(2)}) %all-to-all-start.1) | async-done | bytes 3833888 | tf_op jit(solution)/shard_map/all_to_all | solution.py:183
  498.8 5.4 all-to-all-start.3
  505.4 6.8 bitcast_reduce_fusion.1
  512.5 3.3 gather_fusion
  515.9 1.9 reshape.365
  517.8 3.5 multiply_reduce_fusion.1
  521.4 67.5 %all-to-all-done.3 = bf16[2,32,39,768]{3,0,2,1:T(2,128)(2,1)} async-done(((bf16[2,32,39,768]{3,0,2,1:T(2,128)(2,1)}), bf16[2,32,39,768]{3,0,2,1:T(2,128)(2,1)}, u32[]{:S(2)}, u32[]{:S(2)}) %all-to-all-start.3) | async-done | bytes 3833888 | tf_op jit(solution)/shard_map/all_to_all | solution.py:220
  588.9 6.8 bitcast_reduce_fusion
  596.1 2.2 gather_fusion.1
  601.8 1.9 fusion.48
  604.8 2.7 multiply_reduce_fusion
  610.6 4.2 fusion.56
  614.8 8.8 %fusion.13 = f32[2,768,768]{2,1,0:T(8,128)} fusion(bf16[2,1248,768]{2,1,0:T(8,128)(2,1)} %copy-done.29, bf16[2,1248,768]{2,0,1:T(2,128)(2,1)} %bitcast.12), kind=kOutput, calls=%fused_computation.23 | convolution fusion | flops 2944401408 | bytes 12386304 | tf_op jit(solution)/shard_map/emd,emf->edf/dot_general | solution.py:97
  623.7 11.5 %fusion.7 = f32[2,768,768]{2,1,0:T(8,128)} fusion(bf16[2,1248,768]{2,0,1:T(2,128)(2,1)} %bitcast.16, f32[2,1248,768]{2,1,0:T(8,128)} %copy-done.28), kind=kOutput, calls=%fused_computation.19 | convolution fusion | flops 2961653760 | bytes 16220160 | tf_op jit(solution)/shard_map/emf,emd->efd/dot_general | solution.py:94
  635.4 2.2 fusion.36
  637.7 42.5 %all-reduce.10 = (f32[768]{0:T(1024)S(1)}, f32[768]{0:T(1024)S(1)}, f32[768]{0:T(1024)S(1)}, f32[768]{0:T(1024)S(1)}, f32[768,16]{0,1:T(8,128)S(1)}) all-reduce(f32[768]{0:T(1024)S(1)} %get-tuple-element.15, f32[768]{0:T(1024)S(1)} %get-tuple-element.20, ...), channel_id=2, replica_groups=mesh['expert'=8,'shard'=4] {'expert','shard'}, use_global_device_ids=true, to_apply=%region_24.25.clone | all-reduce | flops 15360 | bytes 122880
  683.2 2.1 fusion.35
  685.4 19.1 %reduce-scatter.6.cloned.1.call-done = f32[24,768]{1,0:T(8,128)} async-done(((f32[768,768]{1,0:T(8,128)}), f32[24,768]{1,0:T(8,128)}) %reduce-scatter.6.cloned.1.call-update) | async-done | bytes 73744 | tf_op jit(solution)/shard_map/reduce_scatter | solution.py:269
  704.5 124.7 %reduce-scatter.4.cloned.1.call-done = f32[24,2304]{1,0:T(8,128)} async-done(((f32[768,2304]{1,0:T(8,128)}), f32[24,2304]{1,0:T(8,128)}) %reduce-scatter.4.cloned.1.call-update) | async-done | bytes 221200 | tf_op jit(solution)/shard_map/reduce_scatter | solution.py:268
  (139 shorter events, 29.9 us)
Async XLA Ops:
  7.2 322.3 %copy-start = (bf16[2,768,768]{2,1,0:T(8,128)(2,1)S(1)}, bf16[2,768,768]{2,1,0:T(8,128)(2,1)}, u32[]{:S(2)}) copy-start(bf16[2,768,768]{2,1,0:T(8,128)(2,1)} %param.22) | copy-start | bytes 7077892
  7.2 66.4 %all-gather.4.cloned.1.call-start = ((), (), s32[]{:S(2)}) async-start(), calls=%async_computation.6 | async-start | bytes 3649536 | tf_op jit(solution)/shard_map/all_gather | solution.py:134
  7.9 121.2 %all-gather.6.cloned.1.call-start = ((), (), s32[]{:S(2)}) async-start(), calls=%async_computation.7 | async-start | bytes 1216512 | tf_op jit(solution)/shard_map/all_gather | solution.py:135
  59.9 13.7 %copy-start.21 = (f32[197]{0:T(256)}, f32[197]{0:T(256)S(1)}, u32[]{:S(2)}) copy-start(f32[197]{0:T(256)S(1)} %add_rsqrt_fusion.1) | copy-start | bytes 2368
  79.1 1.0 copy-start.7
  79.8 1.6 copy-start.4
  79.8 1.6 copy-start.18
  81.4 47.8 %copy-start.6 = (bf16[197,768]{1,0:T(8,128)(2,1)S(1)}, bf16[197,768]{1,0:T(8,128)(2,1)}, u32[]{:S(2)}) copy-start(bf16[197,768]{1,0:T(8,128)(2,1)} %param.12) | copy-start | bytes 907780
  81.4 50.0 %copy-start.23 = (f32[768]{0:T(1024)S(1)}, f32[768]{0:T(1024)}, u32[]{:S(2)}) copy-start(f32[768]{0:T(1024)} %convert_element_type.112) | copy-start | bytes 9220
  83.8 52.3 %copy-start.24 = (s32[394,1]{0,1:T(1,128)S(1)}, s32[394,1]{0,1:T(1,128)}, u32[]{:S(2)}) copy-start(s32[394,1]{0,1:T(1,128)} %compare_select_fusion) | copy-start | bytes 4732
  131.5 0.7 copy-start.9
  148.4 3.7 copy-start.25
  148.4 166.2 %all-to-all-start = ((bf16[2,32,39,768]{3,0,2,1:T(2,128)(2,1)}), bf16[2,32,39,768]{3,0,2,1:T(2,128)(2,1)}, u32[]{:S(2)}, u32[]{:S(2)}) async-start(bf16[2,32,39,768]{3,0,2,1:T(2,128)(2,1)} %bitcast.101), calls=%async_computation | async-start | bytes 7667712 | tf_op jit(solution)/shard_map/all_to_all | solution.py:179
  152.1 152.6 %copy-start.20 = (s32[197,2]{0,1:T(2,128)S(1)}, s32[197,2]{0,1:T(2,128)}, u32[]{:S(2)}) copy-start(s32[197,2]{0,1:T(2,128)} %param.13) | copy-start | bytes 4732
  319.7 88.5 %all-to-all-start.2 = ((bf16[2,32,39,768]{3,0,2,1:T(2,128)(2,1)}), bf16[2,32,39,768]{3,0,2,1:T(2,128)(2,1)}, u32[]{:S(2)}, u32[]{:S(2)}) async-start(bf16[2,32,39,768]{3,0,2,1:T(2,128)(2,1)} %bitcast.102), calls=%async_computation.2 | async-start | bytes 7667712 | tf_op jit(solution)/shard_map/all_to_all | solution.py:214
  329.5 4.9 copy-start.28
  408.2 90.6 %all-to-all-start.1 = ((bf16[2,32,39,768]{3,0,2,1:T(2,128)(2,1)}), bf16[2,32,39,768]{3,0,2,1:T(2,128)(2,1)}, u32[]{:S(2)}, u32[]{:S(2)}) async-start(bf16[2,32,39,768]{3,0,2,1:T(2,128)(2,1)} %bitcast.104), calls=%async_computation.1 | async-start | bytes 7667712 | tf_op jit(solution)/shard_map/all_to_all | solution.py:183
  414.1 10.3 %copy-start.27 = (bf16[2,768,768]{2,1,0:T(8,128)(2,1)S(1)}, bf16[2,768,768]{2,1,0:T(8,128)(2,1)}, u32[]{:S(2)}) copy-start(bf16[2,768,768]{2,1,0:T(8,128)(2,1)} %param.21) | copy-start | bytes 7077892
  424.5 3.5 copy-start.29
  498.8 5.7 copy-start.14
  498.8 90.1 %all-to-all-start.3 = ((bf16[2,32,39,768]{3,0,2,1:T(2,128)(2,1)}), bf16[2,32,39,768]{3,0,2,1:T(2,128)(2,1)}, u32[]{:S(2)}, u32[]{:S(2)}) async-start(bf16[2,32,39,768]{3,0,2,1:T(2,128)(2,1)} %bitcast.103), calls=%async_computation.3 | async-start | bytes 7667712 | tf_op jit(solution)/shard_map/all_to_all | solution.py:220
  504.3 200.2 %reduce-scatter.6.cloned.1.call-start = ((), (), s32[]{:S(2)}) async-start(), calls=%async_computation.9 | async-start | bytes 2433024 | tf_op jit(solution)/shard_map/reduce_scatter | solution.py:269
  512.5 5.3 copy-start.15
  599.1 1.8 copy-start.16
  599.1 2.7 copy-start.17
  601.8 2.8 copy-start.2
  601.8 2.2 copy-start.13
  601.8 3.0 copy-start.19
  603.7 225.4 %reduce-scatter.4.cloned.1.call-start = ((), (), s32[]{:S(2)}) async-start(), calls=%async_computation.8 | async-start | bytes 7299072 | tf_op jit(solution)/shard_map/reduce_scatter | solution.py:268
  604.8 2.8 copy-start.5
  607.5 1.3 copy-start.8
  609.7 0.9 copy-start.22
  610.5 4.3 copy-start.11
  623.7 11.5 %copy-start.10 = (bf16[197,768]{1,0:T(8,128)(2,1)S(1)}, bf16[197,768]{1,0:T(8,128)(2,1)}, u32[]{:S(2)}) copy-start(bf16[197,768]{1,0:T(8,128)(2,1)} %copy-done.9) | copy-start | bytes 907780
  623.7 11.8 %copy-start.12 = (bf16[1,197,3,12,64]{1,4,3,2,0:T(8,128)(2,1)S(1)}, bf16[1,197,3,12,64]{1,4,3,2,0:T(8,128)(2,1)}, u32[]{:S(2)}) copy-start(bf16[1,197,3,12,64]{1,4,3,2,0:T(8,128)(2,1)} %copy-done.11) | copy-start | bytes 2723332
  623.7 11.8 %copy-start.26 = (bf16[768,2304]{1,0:T(8,128)(2,1)S(1)}, bf16[768,2304]{1,0:T(8,128)(2,1)}, u32[]{:S(2)}) copy-start(bf16[768,2304]{1,0:T(8,128)(2,1)} %all-gather.4.cloned.1.call-done) | copy-start | bytes 10616836
  635.2 48.0 %copy-start.3 = (f32[197,768]{1,0:T(8,128)S(1)}, f32[197,768]{1,0:T(8,128)}, u32[]{:S(2)}) copy-start(f32[197,768]{1,0:T(8,128)} %copy-done.2) | copy-start | bytes 1815556
  635.2 193.9 %copy-start.1 = (bf16[2,768,768]{2,1,0:T(8,128)(2,1)S(1)}, bf16[2,768,768]{2,1,0:T(8,128)(2,1)}, u32[]{:S(2)}) copy-start(bf16[2,768,768]{2,1,0:T(8,128)(2,1)} %param.22) | copy-start | bytes 7077892
Sparse Core Ops, SparseCore 0:
  10.8 62.7 all-gather.3
  76.4 52.7 all-gather.5
  603.8 100.5 reduce-scatter.5
  710.6 118.5 reduce-scatter.3
where the time goes:
time: 844 us; the launch traced here: 836 us
  waiting for transfers between devices  386 us (46%)
  blocking collectives  231 us (27%)
  local copies, waits for them, and re-layouts  85 us (10%)
  matrix products  69.3 us (8%)
  other arithmetic  31.1 us (4%)
  starting transfers between devices  19.4 us (2%)
  between operations  14.9 us (2%)
    all_gather x1, blocking collectives, local(): lax.all_gather(w_router, ('expert', 'shard'), axis=0, tiled=True)  146 us
    reduce_scatter x1, waiting for transfers between devices, local(): lax.psum_scatter(grad_qkv, ('expert', 'shard'), scatter_dimension=0, tile...  125 us
    unnamed x2, blocking collectives  84.8 us
    all_to_all x1, waiting for transfers between devices, local(): lax.all_to_all(back_rows.astype(jnp.bfloat16).reshape(EXP_DEV, experts_co...  67.5 us
    all_to_all x1, waiting for transfers between devices, local(): lax.all_to_all(grad_copies, ('expert', 'shard'), split_axis=1, concat_axi...  58.7 us
    all_to_all x1, waiting for transfers between devices, local(): lax.all_to_all(partial_out.astype(jnp.bfloat16).reshape(EXP_DEV, experts_...  55.8 us
    all_gather x1, waiting for transfers between devices, local(): lax.all_gather(w_attn_out, ('expert', 'shard'), axis=0, tiled=True)  45.4 us
    reduce_scatter x1, waiting for transfers between devices, local(): lax.psum_scatter(grad_attn_out, ('expert', 'shard'), scatter_dimension=0,...  19.1 us
  transfers between devices with their start and end apart: 8, of which 7 were waited for; matrix products, arithmetic and copies ran while one was open for 17% of the time, Pallas kernels for 0%

commit v1 on v0

--- a/solution.py
+++ b/solution.py
@@ -9,6 +9,29 @@
 EXP_DEV = 2
 SEQ = 197
 EPS = 1e-06
+
+
+def in_order(pieces, dim):
+    dims = list(pieces.shape[1:])
+    dims[dim] *= pieces.shape[0]
+    return jnp.moveaxis(pieces, 0, dim).reshape(dims)
+
+
+def grow_blocks(shard, axis):
+    length, here = (lax.axis_size(axis), lax.axis_index(axis))
+    blocks, bit = (shard[None], 1)
+    while bit < length:
+        received = lax.ppermute(blocks, axis, [(i, i ^ bit) for i in range(length)])
+        low = here & bit == 0
+        blocks = jnp.concatenate(
+            [jnp.where(low, blocks, received), jnp.where(low, received, blocks)]
+        )
+        bit *= 2
+    return blocks
+
+
+def doubled_up(x, axis, dim):
+    return in_order(grow_blocks(x, axis), dim)
 
 
 def layer_norm(values, gain_vec, bias_vec):
@@ -135,7 +158,7 @@
         lax.all_gather(w_attn_out, ("expert", "shard"), axis=0, tiled=True),
         lax.all_gather(ln2_gain, ("expert", "shard"), axis=0, tiled=True),
         lax.all_gather(ln2_bias, ("expert", "shard"), axis=0, tiled=True),
-        lax.all_gather(w_router, ("expert", "shard"), axis=0, tiled=True),
+        doubled_up(w_router, ("expert", "shard"), 0),
     )
     gain_one = full_ln1_gain.astype(jnp.float32)
     gain_two = full_ln2_gain.astype(jnp.float32)

time: 844 us -> 793 us (0.940)
  blocking collectives: 231 us -> 84.7 us
  waiting for transfers between devices: 386 us -> 472 us
  starting transfers between devices: 19.4 us -> 28.1 us
    all_gather x1 -> x0, blocking collectives: 146 us -> none  [local(): lax.all_gather(w_router, ('expert', 'shard'), axis=0, tiled=True)]
    ppermute x0 -> x5, waiting for transfers between devices: none -> 86.1 us  [grow_blocks(): received = lax.ppermute(blocks, axis, [(i, i ^ bit) for i in range(length)])]
    ppermute x0 -> x5, starting transfers between devices: none -> 8.68 us  [grow_blocks(): received = lax.ppermute(blocks, axis, [(i, i ^ bit) for i in range(length)])]
  transfers between devices with their start and end apart: 8 -> 13, of which waited for: 7 -> 11; matrix products, arithmetic and copies ran while one was open for 17% -> 18% of each run, Pallas kernels for 0% -> 0%
where the time goes in v1:
time: 793 us; the launch traced here: 785 us
  waiting for transfers between devices  472 us (60%)
  local copies, waits for them, and re-layouts  85 us (11%)
  blocking collectives  84.7 us (11%)
  matrix products  69.3 us (9%)
  other arithmetic  31.3 us (4%)
  starting transfers between devices  28.1 us (4%)
  between operations  15 us (2%)
    reduce_scatter x1, waiting for transfers between devices, local(): lax.psum_scatter(grad_qkv, ('expert', 'shard'), scatter_dimension=0, tile...  125 us
    ppermute x5, waiting for transfers between devices, grow_blocks(): received = lax.ppermute(blocks, axis, [(i, i ^ bit) for i in range(length)])  86.1 us
    unnamed x2, blocking collectives  84.7 us
    all_to_all x1, waiting for transfers between devices, local(): lax.all_to_all(back_rows.astype(jnp.bfloat16).reshape(EXP_DEV, experts_co...  67.5 us
    all_to_all x1, waiting for transfers between devices, local(): lax.all_to_all(grad_copies, ('expert', 'shard'), split_axis=1, concat_axi...  58.7 us
    all_to_all x1, waiting for transfers between devices, local(): lax.all_to_all(partial_out.astype(jnp.bfloat16).reshape(EXP_DEV, experts_...  55.8 us
    all_gather x1, waiting for transfers between devices, local(): lax.all_gather(w_attn_out, ('expert', 'shard'), axis=0, tiled=True)  45.4 us
    reduce_scatter x1, waiting for transfers between devices, local(): lax.psum_scatter(grad_attn_out, ('expert', 'shard'), scatter_dimension=0,...  19.1 us
  transfers between devices with their start and end apart: 13, of which 11 were waited for; matrix products, arithmetic and copies ran while one was open for 18% of the time, Pallas kernels for 0%

profile of v1, /device:TPU:0, one launch (start us, length us, event | category | flops | bytes accessed | tf_op | source)
XLA Modules:
  0.0 785.3 jit_solution(2768715452736031312)
XLA Ops:
  13.1 42.3 %all-reduce.11 = (bf16[768]{0:T(1024)(128)(2,1)S(1)}, bf16[768]{0:T(1024)(128)(2,1)S(1)}, bf16[768]{0:T(1024)(128)(2,1)S(1)}, bf16[768]{0:T(1024)(128)(2,1)S(1)}) all-reduce(bf16[768]{0:T(1024)(128)(2,1)S(1)} %dynamic-update-slice.1, bf16[768]{0:T(1024)(128)(2,1)S(1)} %dynamic-update-slice, ...), channel_id=1, replica_groups=mesh['expert'=8,'shard'=4] {'expert','shard'}, use_global_device_ids=true, to_apply=%add.2 | all-reduce | flops 3072 | bytes 12288
  60.5 13.1 %all-gather.3.cloned.1.call-done = bf16[768,2304]{1,0:T(8,128)(2,1)} async-done(((bf16[24,2304]{1,0:T(8,128)(2,1)}), bf16[768,2304]{1,0:T(8,128)(2,1)}) %all-gather.3.cloned.1.call-update) | async-done | bytes 3538960 | tf_op jit(solution)/shard_map/all_gather | solution.py:157
  73.6 4.0 convolution_convert_fusion.2
  81.4 2.4 convolution_convert_fusion.4
  83.8 45.4 %all-gather.5.cloned.1.call-done = bf16[768,768]{1,0:T(8,128)(2,1)} async-done(((bf16[24,768]{1,0:T(8,128)(2,1)}), bf16[768,768]{1,0:T(8,128)(2,1)}) %all-gather.5.cloned.1.call-update) | async-done | bytes 1179664 | tf_op jit(solution)/shard_map/all_gather | solution.py:158
  129.2 1.9 fusion.62
  133.4 2.6 reshape.391
  136.0 3.9 scatter_custom_fusion
  140.0 2.4 broadcast_in_dim.14
  142.4 2.2 copy.124
  144.6 3.9 broadcast_in_dim.15
  148.5 3.7 all-to-all-start
  153.9 61.2 %collective-permute-done = bf16[1,24,16]{1,2,0:T(8,128)(2,1)S(1)} collective-permute-done((bf16[1,24,16]{1,2,0:T(8,128)(2,1)S(1)}, bf16[1,24,16]{1,2,0:T(8,128)(2,1)S(1)}, u32[]{:S(2)}, u32[]{:S(2)}) %collective-permute-start) | collective-permute-done | bytes 800 | tf_op jit(solution)/shard_map/ppermute | solution.py:24
  215.1 5.3 collective-permute-start.1
  220.4 19.9 %collective-permute-done.1 = bf16[2,24,16]{1,2,0:T(8,128)(2,1)S(1)} collective-permute-done((bf16[2,24,16]{1,2,0:T(8,128)(2,1)S(1)}, bf16[2,24,16]{1,2,0:T(8,128)(2,1)S(1)}, u32[]{:S(2)}, u32[]{:S(2)}) %collective-permute-start.1) | collective-permute-done | bytes 1568 | tf_op jit(solution)/shard_map/ppermute | solution.py:24
  241.6 3.9 collective-permute-done.3
  247.1 2.3 mul.285
  249.4 3.0 mul.286
  254.2 4.0 scatter_custom_fusion.1
  258.2 2.4 broadcast_in_dim.16
  260.7 3.1 copy.129
  263.8 5.1 broadcast_in_dim.17
  268.9 3.8 all-to-all-start.2
  272.7 6.0 fusion.15
  278.7 4.9 convolution_convert_fusion.1
  283.6 15.0 %copy.145 = bf16[2,1248,768]{2,0,1:T(2,128)(2,1)} copy(bf16[2,1248,768]{2,1,0:T(8,128)(2,1)S(1)} %convolution_convert_fusion.1) | data formatting | bytes 7667712 | tf_op jit(solution)/shard_map/reshape | solution.py:207
  298.6 58.7 %all-to-all-done.2 = bf16[2,32,39,768]{3,0,2,1:T(2,128)(2,1)} async-done(((bf16[2,32,39,768]{3,0,2,1:T(2,128)(2,1)}), bf16[2,32,39,768]{3,0,2,1:T(2,128)(2,1)}, u32[]{:S(2)}, u32[]{:S(2)}) %all-to-all-start.2) | async-done | bytes 3833888 | tf_op jit(solution)/shard_map/all_to_all | solution.py:237
  357.4 5.9 all-to-all-start.1
  363.3 10.3 %fusion.6 = bf16[2,1248,768]{2,1,0:T(8,128)(2,1)S(1)} fusion(f32[2,1248,768]{2,1,0:T(8,128)} %copy-done.28, bf16[2,768,768]{2,1,0:T(8,128)(2,1)S(1)} %copy-done, bf16[2,1248,768]{2,0,1:T(2,128)(2,1)} %bitcast.16), kind=kOutput, calls=%fused_computation.12 | convolution fusion | flops 2982739968 | bytes 17694720 | tf_op jit(solution)/shard_map/emd,efd->emf/dot_general | solution.py:112
  373.6 3.4 convolution_convert_fusion
  377.1 15.0 %copy.147 = bf16[2,1248,768]{2,0,1:T(2,128)(2,1)} copy(bf16[2,1248,768]{2,1,0:T(8,128)(2,1)S(1)} %convolution_convert_fusion) | data formatting | bytes 7667712 | tf_op jit(solution)/shard_map/reshape | solution.py:244
  392.1 55.8 %all-to-all-done.1 = bf16[2,32,39,768]{3,0,2,1:T(2,128)(2,1)} async-done(((bf16[2,32,39,768]{3,0,2,1:T(2,128)(2,1)}), bf16[2,32,39,768]{3,0,2,1:T(2,128)(2,1)}, u32[]{:S(2)}, u32[]{:S(2)}) %all-to-all-start.1) | async-done | bytes 3833888 | tf_op jit(solution)/shard_map/all_to_all | solution.py:206
  448.0 5.4 all-to-all-start.3
  454.5 6.8 bitcast_reduce_fusion.1
  461.7 3.3 gather_fusion
  467.0 3.5 multiply_reduce_fusion.1
  470.6 67.5 %all-to-all-done.3 = bf16[2,32,39,768]{3,0,2,1:T(2,128)(2,1)} async-done(((bf16[2,32,39,768]{3,0,2,1:T(2,128)(2,1)}), bf16[2,32,39,768]{3,0,2,1:T(2,128)(2,1)}, u32[]{:S(2)}, u32[]{:S(2)}) %all-to-all-start.3) | async-done | bytes 3833888 | tf_op jit(solution)/shard_map/all_to_all | solution.py:243
  538.1 6.8 bitcast_reduce_fusion
  545.3 2.2 gather_fusion.1
  553.9 2.7 multiply_reduce_fusion
  559.7 4.2 fusion.56
  564.0 8.8 %fusion.13 = f32[2,768,768]{2,1,0:T(8,128)} fusion(bf16[2,1248,768]{2,1,0:T(8,128)(2,1)} %copy-done.29, bf16[2,1248,768]{2,0,1:T(2,128)(2,1)} %bitcast.12), kind=kOutput, calls=%fused_computation.23 | convolution fusion | flops 2944401408 | bytes 12386304 | tf_op jit(solution)/shard_map/emd,emf->edf/dot_general | solution.py:120
  572.8 11.5 %fusion.7 = f32[2,768,768]{2,1,0:T(8,128)} fusion(bf16[2,1248,768]{2,0,1:T(2,128)(2,1)} %bitcast.16, f32[2,1248,768]{2,1,0:T(8,128)} %copy-done.28), kind=kOutput, calls=%fused_computation.19 | convolution fusion | flops 2961653760 | bytes 16220160 | tf_op jit(solution)/shard_map/emf,emd->efd/dot_general | solution.py:117
  584.6 2.2 fusion.36
  586.8 42.5 %all-reduce.10 = (f32[768]{0:T(1024)S(1)}, f32[768]{0:T(1024)S(1)}, f32[768]{0:T(1024)S(1)}, f32[768]{0:T(1024)S(1)}, f32[768,16]{0,1:T(8,128)S(1)}) all-reduce(f32[768]{0:T(1024)S(1)} %get-tuple-element.15, f32[768]{0:T(1024)S(1)} %get-tuple-element.20, ...), channel_id=2, replica_groups=mesh['expert'=8,'shard'=4] {'expert','shard'}, use_global_device_ids=true, to_apply=%region_24.25.clone | all-reduce | flops 15360 | bytes 122880
  632.4 2.1 fusion.35
  634.5 19.1 %reduce-scatter.6.cloned.1.call-done = f32[24,768]{1,0:T(8,128)} async-done(((f32[768,768]{1,0:T(8,128)}), f32[24,768]{1,0:T(8,128)}) %reduce-scatter.6.cloned.1.call-update) | async-done | bytes 73744 | tf_op jit(solution)/shard_map/reduce_scatter | solution.py:292
  653.6 124.7 %reduce-scatter.4.cloned.1.call-done = f32[24,2304]{1,0:T(8,128)} async-done(((f32[768,2304]{1,0:T(8,128)}), f32[24,2304]{1,0:T(8,128)}) %reduce-scatter.4.cloned.1.call-update) | async-done | bytes 221200 | tf_op jit(solution)/shard_map/reduce_scatter | solution.py:291
  (158 shorter events, 40.0 us)
Async XLA Ops:
  7.2 271.5 %copy-start = (bf16[2,768,768]{2,1,0:T(8,128)(2,1)S(1)}, bf16[2,768,768]{2,1,0:T(8,128)(2,1)}, u32[]{:S(2)}) copy-start(bf16[2,768,768]{2,1,0:T(8,128)(2,1)} %param.22) | copy-start | bytes 7077892
  7.2 66.4 %all-gather.3.cloned.1.call-start = ((), (), s32[]{:S(2)}) async-start(), calls=%async_computation.6 | async-start | bytes 3649536 | tf_op jit(solution)/shard_map/all_gather | solution.py:157
  7.9 121.2 %all-gather.5.cloned.1.call-start = ((), (), s32[]{:S(2)}) async-start(), calls=%async_computation.7 | async-start | bytes 1216512 | tf_op jit(solution)/shard_map/all_gather | solution.py:158
  59.9 13.7 %copy-start.21 = (f32[197]{0:T(256)}, f32[197]{0:T(256)S(1)}, u32[]{:S(2)}) copy-start(f32[197]{0:T(256)S(1)} %add_rsqrt_fusion.1) | copy-start | bytes 2368
  79.1 1.0 copy-start.7
  79.8 1.6 copy-start.4
  79.8 1.6 copy-start.18
  81.4 47.8 %copy-start.6 = (bf16[197,768]{1,0:T(8,128)(2,1)S(1)}, bf16[197,768]{1,0:T(8,128)(2,1)}, u32[]{:S(2)}) copy-start(bf16[197,768]{1,0:T(8,128)(2,1)} %param.12) | copy-start | bytes 907780
  81.4 50.0 %copy-start.23 = (f32[768]{0:T(1024)S(1)}, f32[768]{0:T(1024)}, u32[]{:S(2)}) copy-start(f32[768]{0:T(1024)} %convert_element_type.112) | copy-start | bytes 9220
  83.8 52.3 %copy-start.24 = (s32[394,1]{0,1:T(1,128)S(1)}, s32[394,1]{0,1:T(1,128)}, u32[]{:S(2)}) copy-start(s32[394,1]{0,1:T(1,128)} %compare_select_fusion) | copy-start | bytes 4732
  131.5 0.7 copy-start.9
  148.5 3.7 copy-start.25
  148.5 115.3 %all-to-all-start = ((bf16[2,32,39,768]{3,0,2,1:T(2,128)(2,1)}), bf16[2,32,39,768]{3,0,2,1:T(2,128)(2,1)}, u32[]{:S(2)}, u32[]{:S(2)}) async-start(bf16[2,32,39,768]{3,0,2,1:T(2,128)(2,1)} %bitcast.103), calls=%async_computation | async-start | bytes 7667712 | tf_op jit(solution)/shard_map/all_to_all | solution.py:202
  152.2 101.8 %copy-start.20 = (s32[197,2]{0,1:T(2,128)S(1)}, s32[197,2]{0,1:T(2,128)}, u32[]{:S(2)}) copy-start(s32[197,2]{0,1:T(2,128)} %param.13) | copy-start | bytes 4732
  152.2 62.9 %collective-permute-start = (bf16[1,24,16]{1,2,0:T(8,128)(2,1)S(1)}, bf16[1,24,16]{1,2,0:T(8,128)(2,1)S(1)}, u32[]{:S(2)}, u32[]{:S(2)}) collective-permute-start(bf16[1,24,16]{1,2,0:T(8,128)(2,1)S(1)} %bitcast.122), channel_id=1, source_target_pairs={{0,1},{1,0},{2,3},{3,2},{4,5},{5,4},{6,7},{7,6},{8,9},{9,8},{10,11... | collective-permute-start | bytes 2312 | tf_op jit(solution)/shard_map/ppermute | solution.py:24
  215.1 25.1 %collective-permute-start.1 = (bf16[2,24,16]{1,2,0:T(8,128)(2,1)S(1)}, bf16[2,24,16]{1,2,0:T(8,128)(2,1)S(1)}, u32[]{:S(2)}, u32[]{:S(2)}) collective-permute-start(bf16[2,24,16]{1,2,0:T(8,128)(2,1)S(1)} %pad_maximum_fusion.5), channel_id=1, source_target_pairs={{0,2},{1,3},{2,0},{3,1},{4,6},{5,7},{6,4},{7,5},{8,10},{9,11},{10,... | collective-permute-start | bytes 4616 | tf_op jit(solution)/shard_map/ppermute | solution.py:24
  240.3 1.2 collective-permute-start.2
  241.5 4.0 collective-permute-start.3
  245.6 6.8 collective-permute-start.4
  268.9 88.5 %all-to-all-start.2 = ((bf16[2,32,39,768]{3,0,2,1:T(2,128)(2,1)}), bf16[2,32,39,768]{3,0,2,1:T(2,128)(2,1)}, u32[]{:S(2)}, u32[]{:S(2)}) async-start(bf16[2,32,39,768]{3,0,2,1:T(2,128)(2,1)} %bitcast.104), calls=%async_computation.2 | async-start | bytes 7667712 | tf_op jit(solution)/shard_map/all_to_all | solution.py:237
  278.7 4.9 copy-start.28
  357.4 90.6 %all-to-all-start.1 = ((bf16[2,32,39,768]{3,0,2,1:T(2,128)(2,1)}), bf16[2,32,39,768]{3,0,2,1:T(2,128)(2,1)}, u32[]{:S(2)}, u32[]{:S(2)}) async-start(bf16[2,32,39,768]{3,0,2,1:T(2,128)(2,1)} %bitcast.106), calls=%async_computation.1 | async-start | bytes 7667712 | tf_op jit(solution)/shard_map/all_to_all | solution.py:206
  363.3 10.3 %copy-start.27 = (bf16[2,768,768]{2,1,0:T(8,128)(2,1)S(1)}, bf16[2,768,768]{2,1,0:T(8,128)(2,1)}, u32[]{:S(2)}) copy-start(bf16[2,768,768]{2,1,0:T(8,128)(2,1)} %param.21) | copy-start | bytes 7077892
  373.6 3.5 copy-start.29
  448.0 5.7 copy-start.14
  448.0 90.1 %all-to-all-start.3 = ((bf16[2,32,39,768]{3,0,2,1:T(2,128)(2,1)}), bf16[2,32,39,768]{3,0,2,1:T(2,128)(2,1)}, u32[]{:S(2)}, u32[]{:S(2)}) async-start(bf16[2,32,39,768]{3,0,2,1:T(2,128)(2,1)} %bitcast.105), calls=%async_computation.3 | async-start | bytes 7667712 | tf_op jit(solution)/shard_map/all_to_all | solution.py:243
  453.4 200.2 %reduce-scatter.6.cloned.1.call-start = ((), (), s32[]{:S(2)}) async-start(), calls=%async_computation.9 | async-start | bytes 2433024 | tf_op jit(solution)/shard_map/reduce_scatter | solution.py:292
  461.7 5.3 copy-start.15
  548.2 1.8 copy-start.16
  548.2 2.7 copy-start.17
  550.9 2.8 copy-start.2
  550.9 2.2 copy-start.13
  551.0 3.0 copy-start.19
  552.9 225.4 %reduce-scatter.4.cloned.1.call-start = ((), (), s32[]{:S(2)}) async-start(), calls=%async_computation.8 | async-start | bytes 7299072 | tf_op jit(solution)/shard_map/reduce_scatter | solution.py:291
  553.9 2.8 copy-start.5
  556.7 1.3 copy-start.8
  558.8 0.9 copy-start.22
  559.7 4.3 copy-start.11
  572.8 11.5 %copy-start.10 = (bf16[197,768]{1,0:T(8,128)(2,1)S(1)}, bf16[197,768]{1,0:T(8,128)(2,1)}, u32[]{:S(2)}) copy-start(bf16[197,768]{1,0:T(8,128)(2,1)} %copy-done.9) | copy-start | bytes 907780
  572.8 11.8 %copy-start.12 = (bf16[1,197,3,12,64]{1,4,3,2,0:T(8,128)(2,1)S(1)}, bf16[1,197,3,12,64]{1,4,3,2,0:T(8,128)(2,1)}, u32[]{:S(2)}) copy-start(bf16[1,197,3,12,64]{1,4,3,2,0:T(8,128)(2,1)} %copy-done.11) | copy-start | bytes 2723332
  572.8 11.8 %copy-start.26 = (bf16[768,2304]{1,0:T(8,128)(2,1)S(1)}, bf16[768,2304]{1,0:T(8,128)(2,1)}, u32[]{:S(2)}) copy-start(bf16[768,2304]{1,0:T(8,128)(2,1)} %all-gather.3.cloned.1.call-done) | copy-start | bytes 10616836
  584.4 48.0 %copy-start.3 = (f32[197,768]{1,0:T(8,128)S(1)}, f32[197,768]{1,0:T(8,128)}, u32[]{:S(2)}) copy-start(f32[197,768]{1,0:T(8,128)} %copy-done.2) | copy-start | bytes 1815556
  584.4 193.9 %copy-start.1 = (bf16[2,768,768]{2,1,0:T(8,128)(2,1)S(1)}, bf16[2,768,768]{2,1,0:T(8,128)(2,1)}, u32[]{:S(2)}) copy-start(bf16[2,768,768]{2,1,0:T(8,128)(2,1)} %param.22) | copy-start | bytes 7077892
Sparse Core Ops, SparseCore 0:
  10.8 62.7 all-gather.2
  76.4 52.7 all-gather.4
  553.0 100.5 reduce-scatter.5
  659.7 118.5 reduce-scatter.3
